TPU v7x, 32 devices: a whole 2x2x4 slice. The times are simulated.
32 devices in a mesh: row: 4 (over z), col: 8 (over y, x, core).
Axes of the slice: x: 2, y: 2, z: 4, core: 2. Of those that a mesh axis runs over, the one named last changes fastest.
Arguments:
- factor_panel: bfloat16 [1024, 8192], P('row', 'col'), may hold values from -0.1875 to 0.1875
- ancestor_inv: float32 [1024, 1024], P('row', 'col'), may hold values from -6 to 6
- diag_inverse: float32 [4096, 8192], P('row', 'col'), may hold values from -6 to 6
- structure: int32 [2, 4], replicated, may hold values 0 or 1
Outputs:
- inverse_panel: float32 [1024, 8192], P('row', 'col')
- diag_sigma: float32 [4096, 8192], P('row', 'col')
All inputs are finite; a program needn't handle non-finite values.
Results may differ from a plain program's by a relative error of at most 0.0003.
Values may be sent and summed in bfloat16 or wider, within the bound.
A program may use at most 128 MiB of HBM per device.

v0:
```python
import jax
import jax.numpy as jnp
from jax import lax
from jax.sharding import PartitionSpec as P

B = 256
NS = 2


def local(factor_panel, ancestor_inv, diag_inverse, structure):
    rows_dev, width_dev = factor_panel.shape
    per_block = width_dev // NS
    row_index = lax.axis_index("row")
    keep_tiles = jnp.repeat(structure, B, axis=1)
    keep_own = lax.dynamic_slice_in_dim(keep_tiles, row_index * rows_dev, rows_dev, 1)
    keep_cols = jnp.repeat(keep_own.T, per_block, axis=1)
    lhat_local = jnp.where(keep_cols == 1, factor_panel, jnp.zeros_like(factor_panel))
    column = lax.all_gather(lhat_local, "row", axis=0, tiled=True)
    sigma_rows = lax.all_gather(ancestor_inv, "col", axis=1, tiled=True)
    column_wide = column.astype(jnp.float32)
    running = jnp.dot(sigma_rows, column_wide, precision=lax.Precision.HIGHEST)
    inverse_panel = jnp.where(keep_cols == 1, -running, jnp.zeros_like(running))
    rows_all = lax.all_gather(lhat_local, "col", axis=1, tiled=True)
    block_count = rows_all.shape[1] // width_dev
    rows_cube = rows_all.reshape(rows_dev, block_count, NS, per_block)
    lhat_members = [
        rows_cube[:, :, member, :].reshape(rows_dev, block_count * per_block).astype(jnp.float32)
        for member in range(NS)
    ]
    pieces = []
    for member in range(NS):
        window = lhat_members[member]
        target = inverse_panel[:, member * per_block : (member + 1) * per_block]
        pieces.append(
            lax.dot_general(
                window,
                target,
                (((0,), (0,)), ((), ())),
                precision=lax.Precision.HIGHEST,
                preferred_element_type=jnp.float32,
            )
        )
    update = lax.psum_scatter(
        jnp.concatenate(pieces, axis=1), "row", scatter_dimension=0, tiled=True
    )
    diag_sigma = diag_inverse - update
    return (inverse_panel, diag_sigma)


def solution(mesh):
    placed = (P("row", "col"), P("row", "col"), P("row", "col"), P())
    return jax.shard_map(
        local,
        mesh=mesh,
        in_specs=placed,
        out_specs=(P("row", "col"), P("row", "col")),
        check_vma=False,
    )
```

profile of v0, /device:TPU:0, one launch (start us, length us, event | category | flops | bytes accessed | tf_op | source)
XLA Modules:
  0.0 437.1 jit_solution(3430236630493984573)
XLA Ops:
  7.2 0.0 all-gather.6.cloned.1.call-start
  7.2 0.7 all-gather.6.cloned.1.call-update
  7.9 0.0 all-gather.4.cloned.1.call-start
  8.0 0.1 broadcast_bitcast_fusion
  8.1 1.2 copy.6
  9.3 0.8 bitcast_select_fusion.1
  10.2 0.0 all-gather.4.cloned.1.call-update
  10.2 0.0 all-gather.8.cloned.1.call-start
  10.2 0.7 all-gather.8.cloned.1.call-update
  10.9 0.0 reduce-scatter.2.cloned.1.call-start
  11.0 25.2 %all-gather.6.cloned.1.call-done = f32[256,1024]{1,0:T(8,128)} async-done(((f32[256,128]{1,0:T(8,128)}), f32[256,1024]{1,0:T(8,128)}) %all-gather.6.cloned.1.call-update) | async-done | bytes 1048592 | tf_op jit(solution)/shard_map/all_gather | solution.py:19
  36.2 48.4 %all-gather.4.cloned.1.call-done = bf16[1024,1024]{0,1:T(8,128)(2,1)} async-done(((bf16[256,1024]{0,1:T(8,128)(2,1)}), bf16[1024,1024]{0,1:T(8,128)(2,1)}) %all-gather.4.cloned.1.call-update) | async-done | bytes 2097168 | tf_op jit(solution)/shard_map/all_gather | solution.py:18
  84.6 3.7 bitcast_select_fusion
  88.3 33.7 %all-gather.8.cloned.1.call-done = bf16[256,8192]{0,1:T(8,128)(2,1)} async-done(((bf16[256,1024]{0,1:T(8,128)(2,1)}), bf16[256,8192]{0,1:T(8,128)(2,1)}) %all-gather.8.cloned.1.call-update) | async-done | bytes 4194320 | tf_op jit(solution)/shard_map/all_gather | solution.py:23
  122.1 2.6 fusion.5
  124.6 3.5 fusion.1
  128.1 3.5 fusion.3
  131.6 6.4 %pad_maximum_fusion = f32[4096,1024]{0,1:T(8,128)} fusion(f32[4096,512]{0,1:T(8,128)S(1)} %fusion.1, f32[4096,512]{0,1:T(8,128)S(1)} %fusion.3), kind=kLoop, calls=%fused_computation | loop fusion | flops 4194304 | bytes 33554432 | tf_op jit(solution)/shard_map/concatenate | solution.py:44
  138.0 0.0 reduce-scatter.2.cloned.1.call-update
  138.0 5.3 %copy.7 = f32[1024,1024]{0,1:T(8,128)} copy(f32[1024,1024]{1,0:T(8,128)} %param.6) | data formatting | bytes 8388608 | tf_op args[2]
  143.3 1.3 copy.8
  144.6 273.8 %reduce-scatter.2.cloned.1.call-done = f32[1024,1024]{0,1:T(8,128)} async-done(((f32[4096,1024]{0,1:T(8,128)}), f32[1024,1024]{0,1:T(8,128)}) %reduce-scatter.2.cloned.1.call-update) | async-done | bytes 4194320 | tf_op jit(solution)/shard_map/reduce_scatter | solution.py:43
  418.4 6.8 %sub.3 = f32[1024,1024]{0,1:T(8,128)} subtract(f32[1024,1024]{0,1:T(8,128)} %copy.7, f32[1024,1024]{0,1:T(8,128)} %reduce-scatter.2.cloned.1.call-done) | non-fusion elementwise | flops 1048576 | bytes 12582912 | tf_op jit(solution)/shard_map/sub | solution.py:46
  425.2 5.3 %copy.9 = f32[1024,1024]{1,0:T(8,128)} copy(f32[1024,1024]{0,1:T(8,128)} %sub.3) | data formatting | bytes 8388608
  (6 shorter events, 0.0 us)
Async XLA Ops:
  7.2 0.8 copy-start
  7.2 29.0 %all-gather.6.cloned.1.call-start = ((), (), s32[]{:S(2)}) async-start(), calls=%async_computation.2 | async-start | bytes 1179648 | tf_op jit(solution)/shard_map/all_gather | solution.py:19
  7.9 76.7 %all-gather.4.cloned.1.call-start = ((), (), s32[]{:S(2)}) async-start(), calls=%async_computation.1 | async-start | bytes 2621440 | tf_op jit(solution)/shard_map/all_gather | solution.py:18
  10.2 111.9 %all-gather.8.cloned.1.call-start = ((), (), s32[]{:S(2)}) async-start(), calls=%async_computation.3 | async-start | bytes 4718592 | tf_op jit(solution)/shard_map/all_gather | solution.py:23
  10.9 407.5 %reduce-scatter.2.cloned.1.call-start = ((), (), s32[]{:S(2)}) async-start(), calls=%async_computation.4 | async-start | bytes 20971520 | tf_op jit(solution)/shard_map/reduce_scatter | solution.py:43
  418.4 12.1 %copy-start.1 = (s32[2,4]{1,0:T(2,128)S(1)}, s32[2,4]{1,0:T(2,128)}, u32[]{:S(2)}) copy-start(s32[2,4]{1,0:T(2,128)} %param.7) | copy-start | bytes 100
Sparse Core Ops, SparseCore 0:
  9.9 26.2 all-gather.5
  38.3 46.2 all-gather.3
  87.1 34.9 all-gather.7
  138.1 280.2 reduce-scatter.1
where the time goes:
time: 437 us
  waiting for transfers between devices  383 us (88%)
  local copies, waits for them, and re-layouts  15.9 us (4%)
  other arithmetic  14 us (3%)
  between operations  13.8 us (3%)
  matrix products  10.6 us (2%)
    reduce_scatter x1, waiting for transfers between devices, local(): lax.psum_scatter(jnp.concatenate(pieces, axis=1), 'row', scatter_dimensio...  274 us
    all_gather x1, waiting for transfers between devices, local(): column = lax.all_gather(lhat_local, 'row', axis=0, tiled=True)  48.4 us
    all_gather x1, waiting for transfers between devices, local(): rows_all = lax.all_gather(lhat_local, 'col', axis=1, tiled=True)  33.7 us
    all_gather x1, waiting for transfers between devices, local(): sigma_rows = lax.all_gather(ancestor_inv, 'col', axis=1, tiled=True)  25.2 us
    unnamed x10, local copies, waits for them, and re-layouts  13.3 us
  transfers between devices with their start and end apart: 4, of which 4 were waited for; matrix products, arithmetic and copies ran while one was open for 3% of the time, Pallas kernels for 0%

commit v1 on v0

--- a/solution.py
+++ b/solution.py
@@ -5,6 +5,18 @@
 
 B = 256
 NS = 2
+
+
+def collect(x, axis, dim):
+    ways, here, lap = (lax.axis_size(axis), lax.axis_index(axis), x.shape[dim])
+    line, have = (x, 1)
+    while have < ways:
+        line = jnp.concatenate(
+            [line, lax.ppermute(line, axis, [(d, (d - have) % ways) for d in range(ways)])],
+            axis=dim,
+        )
+        have = 2 * have
+    return jnp.roll(line, here * lap, axis=dim)
 
 
 def local(factor_panel, ancestor_inv, diag_inverse, structure):
@@ -16,7 +28,7 @@
     keep_cols = jnp.repeat(keep_own.T, per_block, axis=1)
     lhat_local = jnp.where(keep_cols == 1, factor_panel, jnp.zeros_like(factor_panel))
     column = lax.all_gather(lhat_local, "row", axis=0, tiled=True)
-    sigma_rows = lax.all_gather(ancestor_inv, "col", axis=1, tiled=True)
+    sigma_rows = collect(ancestor_inv, "col", 1)
     column_wide = column.astype(jnp.float32)
     running = jnp.dot(sigma_rows, column_wide, precision=lax.Precision.HIGHEST)
     inverse_panel = jnp.where(keep_cols == 1, -running, jnp.zeros_like(running))

time: 437 us -> 412 us (0.943)
  waiting for transfers between devices: 383 us -> 352 us
  starting transfers between devices: 0.16 us -> 4.68 us
    all_gather x1, waiting for transfers between devices: 48.4 us -> 18.8 us  [local(): column = lax.all_gather(lhat_local, 'row', axis=0, tiled=True)]
    all_gather x1 -> x0, waiting for transfers between devices: 25.2 us -> none  [local(): sigma_rows = lax.all_gather(ancestor_inv, 'col', axis=1, tiled=True)]
    ppermute x0 -> x3, waiting for transfers between devices: none -> 23.4 us  [collect(): lax.ppermute(line, axis, [(d, (d - have) % ways) for d in range(ways)])]
    ppermute x0 -> x3, starting transfers between devices: none -> 4.57 us  [collect(): lax.ppermute(line, axis, [(d, (d - have) % ways) for d in range(ways)])]
    unnamed x10 -> x20, local copies, waits for them, and re-layouts: 13.3 us -> 12.8 us
  transfers between devices with their start and end apart: 4 -> 6, of which waited for: 4 -> 6; matrix products, arithmetic and copies ran while one was open for 3% -> 2% of each run, Pallas kernels for 0% -> 0%
where the time goes in v1:
time: 412 us
  waiting for transfers between devices  352 us (85%)
  local copies, waits for them, and re-layouts  15.8 us (4%)
  other arithmetic  14.9 us (4%)
  between operations  13.9 us (3%)
  matrix products  10.4 us (3%)
  starting transfers between devices  4.68 us (1%)
    reduce_scatter x1, waiting for transfers between devices, local(): lax.psum_scatter(jnp.concatenate(pieces, axis=1), 'row', scatter_dimensio...  275 us
    all_gather x1, waiting for transfers between devices, local(): rows_all = lax.all_gather(lhat_local, 'col', axis=1, tiled=True)  34 us
    ppermute x3, waiting for transfers between devices, collect(): lax.ppermute(line, axis, [(d, (d - have) % ways) for d in range(ways)])  23.4 us
    all_gather x1, waiting for transfers between devices, local(): column = lax.all_gather(lhat_local, 'row', axis=0, tiled=True)  18.8 us
    unnamed x20, local copies, waits for them, and re-layouts  12.8 us
  transfers between devices with their start and end apart: 6, of which 6 were waited for; matrix products, arithmetic and copies ran while one was open for 2% of the time, Pallas kernels for 0%

profile of v1, /device:TPU:0, one launch (start us, length us, event | category | flops | bytes accessed | tf_op | source)
XLA Modules:
  0.0 411.7 jit_solution(14703678888712289766)
XLA Ops:
  7.2 0.6 copy-done
  7.9 1.2 copy.9
  9.2 0.8 bitcast_select_fusion
  10.1 0.7 all-gather.5.cloned.1.call-update
  10.9 3.4 collective-permute-start
  14.3 2.5 collective-permute-done
  16.8 0.6 collective-permute-start.1
  17.4 8.1 %collective-permute-done.1 = f32[256,256]{1,0:T(8,128)S(1)} collective-permute-done((f32[256,256]{1,0:T(8,128)S(1)}, f32[256,256]{1,0:T(8,128)S(1)}, u32[]{:S(2)}, u32[]{:S(2)}) %collective-permute-start.1) | collective-permute-done | bytes 262176 | tf_op jit(solution)/shard_map/ppermute | solution.py:15
  25.5 0.9 pad_maximum_fusion.1
  26.4 0.6 collective-permute-start.2
  26.9 0.1 broadcast_in_dim.13
  27.0 0.3 copy.10
  27.4 12.8 %collective-permute-done.2 = f32[256,512]{1,0:T(8,128)S(1)} collective-permute-done((f32[256,512]{1,0:T(8,128)}, f32[256,512]{1,0:T(8,128)S(1)}, u32[]{:S(2)}, u32[]{:S(2)}) %collective-permute-start.2) | collective-permute-done | bytes 524320 | tf_op jit(solution)/shard_map/ppermute | solution.py:15
  40.4 18.8 %all-gather.3.cloned.1.call-done = bf16[1024,1024]{0,1:T(8,128)(2,1)} async-done(((bf16[256,1024]{0,1:T(8,128)(2,1)}), bf16[1024,1024]{0,1:T(8,128)(2,1)}) %all-gather.3.cloned.1.call-update) | async-done | bytes 2097168 | tf_op jit(solution)/shard_map/all_gather | solution.py:30
  59.1 3.5 fusion
  62.6 34.0 %all-gather.5.cloned.1.call-done = bf16[256,8192]{0,1:T(8,128)(2,1)} async-done(((bf16[256,1024]{0,1:T(8,128)(2,1)}), bf16[256,8192]{0,1:T(8,128)(2,1)}) %all-gather.5.cloned.1.call-update) | async-done | bytes 4194320 | tf_op jit(solution)/shard_map/all_gather | solution.py:35
  96.6 2.6 fusion.7
  99.2 3.5 fusion.2
  102.7 3.5 fusion.4
  106.2 6.4 %pad_maximum_fusion = f32[4096,1024]{0,1:T(8,128)} fusion(f32[4096,512]{0,1:T(8,128)S(1)} %fusion.2, f32[4096,512]{0,1:T(8,128)S(1)} %fusion.4), kind=kLoop, calls=%fused_computation | loop fusion | flops 4194304 | bytes 33554432 | tf_op jit(solution)/shard_map/concatenate | solution.py:56
  112.6 5.3 %copy.13 = f32[1024,1024]{0,1:T(8,128)} copy(f32[1024,1024]{1,0:T(8,128)} %param.6) | data formatting | bytes 8388608 | tf_op args[2]
  117.9 275.1 %reduce-scatter.2.cloned.1.call-done = f32[1024,1024]{0,1:T(8,128)} async-done(((f32[4096,1024]{0,1:T(8,128)}), f32[1024,1024]{0,1:T(8,128)}) %reduce-scatter.2.cloned.1.call-update) | async-done | bytes 4194320 | tf_op jit(solution)/shard_map/reduce_scatter | solution.py:55
  393.0 6.8 %sub.8 = f32[1024,1024]{0,1:T(8,128)} subtract(f32[1024,1024]{0,1:T(8,128)} %copy.13, f32[1024,1024]{0,1:T(8,128)} %reduce-scatter.2.cloned.1.call-done) | non-fusion elementwise | flops 1048576 | bytes 12582912 | tf_op jit(solution)/shard_map/sub | solution.py:58
  399.8 5.3 %copy.14 = f32[1024,1024]{1,0:T(8,128)} copy(f32[1024,1024]{0,1:T(8,128)} %sub.8) | data formatting | bytes 8388608
  (24 shorter events, 0.5 us)
Async XLA Ops:
  7.2 0.7 copy-start
  7.2 3.7 copy-start.3
  7.2 52.0 %all-gather.3.cloned.1.call-start = ((), (), s32[]{:S(2)}) async-start(), calls=%async_computation.1 | async-start | bytes 2621440 | tf_op jit(solution)/shard_map/all_gather | solution.py:30
  10.1 86.5 %all-gather.5.cloned.1.call-start = ((), (), s32[]{:S(2)}) async-start(), calls=%async_computation.2 | async-start | bytes 4718592 | tf_op jit(solution)/shard_map/all_gather | solution.py:35
  10.8 382.2 %reduce-scatter.2.cloned.1.call-start = ((), (), s32[]{:S(2)}) async-start(), calls=%async_computation.3 | async-start | bytes 20971520 | tf_op jit(solution)/shard_map/reduce_scatter | solution.py:55
  10.9 5.9 %collective-permute-start = (f32[256,128]{1,0:T(8,128)S(1)}, f32[256,128]{1,0:T(8,128)S(1)}, u32[]{:S(2)}, u32[]{:S(2)}) collective-permute-start(f32[256,128]{1,0:T(8,128)S(1)} %copy-done.3), channel_id=1, source_target_pairs={{0,7},{1,0},{2,1},{3,2},{4,3},{5,4},{6,5},{7,6},{8,15},{9,8},{10,9... | collective-permute-start | bytes 393224 | tf_op jit(solution)/shard_map/ppermute | solution.py:15
  16.8 8.7 %collective-permute-start.1 = (f32[256,256]{1,0:T(8,128)S(1)}, f32[256,256]{1,0:T(8,128)S(1)}, u32[]{:S(2)}, u32[]{:S(2)}) collective-permute-start(f32[256,256]{1,0:T(8,128)S(1)} %pad_maximum_fusion.2), channel_id=1, source_target_pairs={{0,6},{1,7},{2,0},{3,1},{4,2},{5,3},{6,4},{7,5},{8,14},{9,15},{10,... | collective-permute-start | bytes 786440 | tf_op jit(solution)/shard_map/ppermute | solution.py:15
  26.4 13.8 %collective-permute-start.2 = (f32[256,512]{1,0:T(8,128)}, f32[256,512]{1,0:T(8,128)S(1)}, u32[]{:S(2)}, u32[]{:S(2)}) collective-permute-start(f32[256,512]{1,0:T(8,128)} %pad_maximum_fusion.1), channel_id=1, source_target_pairs={{0,4},{1,5},{2,6},{3,7},{4,0},{5,1},{6,2},{7,3},{8,12},{9,13},{10,... | collective-permute-start | bytes 1572872 | tf_op jit(solution)/shard_map/ppermute | solution.py:15
  62.6 40.1 %copy-start.2 = (f32[256,1024]{1,0:T(8,128)}, f32[256,1024]{1,0:T(8,128)S(1)}, u32[]{:S(2)}) copy-start(f32[256,1024]{1,0:T(8,128)S(1)} %fusion) | copy-start | bytes 3145732
  399.8 5.4 %copy-start.1 = (s32[2,4]{1,0:T(2,128)S(1)}, s32[2,4]{1,0:T(2,128)}, u32[]{:S(2)}) copy-start(s32[2,4]{1,0:T(2,128)} %param.7) | copy-start | bytes 100
Sparse Core Ops, SparseCore 0:
  10.2 48.9 all-gather.2
  61.6 34.9 all-gather.4
  112.7 280.2 reduce-scatter.1

commit v2 on v0

--- a/solution.py
+++ b/solution.py
@@ -5,6 +5,24 @@
 
 B = 256
 NS = 2
+
+
+def collect(array, axis, dim):
+    ways, here, step = (lax.axis_size(axis), lax.axis_index(axis), array.shape[dim])
+    lengths = [n * ways if d == dim else n for d, n in enumerate(array.shape)]
+    full = lax.dynamic_update_slice_in_dim(
+        jnp.zeros(lengths, array.dtype), array, here * step, axis=dim
+    )
+    going_up = going_down = array
+    for far in range(1, ways // 2 + 1):
+        going_up = lax.ppermute(going_up, axis, [(d, (d + 1) % ways) for d in range(ways)])
+        full = lax.dynamic_update_slice_in_dim(full, going_up, (here - far) % ways * step, axis=dim)
+        if 2 * far < ways:
+            going_down = lax.ppermute(going_down, axis, [(d, (d - 1) % ways) for d in range(ways)])
+            full = lax.dynamic_update_slice_in_dim(
+                full, going_down, (here + far) % ways * step, axis=dim
+            )
+    return full
 
 
 def local(factor_panel, ancestor_inv, diag_inverse, structure):
@@ -15,7 +33,7 @@
     keep_own = lax.dynamic_slice_in_dim(keep_tiles, row_index * rows_dev, rows_dev, 1)
     keep_cols = jnp.repeat(keep_own.T, per_block, axis=1)
     lhat_local = jnp.where(keep_cols == 1, factor_panel, jnp.zeros_like(factor_panel))
-    column = lax.all_gather(lhat_local, "row", axis=0, tiled=True)
+    column = collect(lhat_local, "row", 0)
     sigma_rows = lax.all_gather(ancestor_inv, "col", axis=1, tiled=True)
     column_wide = column.astype(jnp.float32)
     running = jnp.dot(sigma_rows, column_wide, precision=lax.Precision.HIGHEST)

time: 437 us -> 391 us (0.89)
  waiting for transfers between devices: 383 us -> 330 us
  starting transfers between devices: 0.16 us -> 5.29 us
    all_gather x1 -> x0, waiting for transfers between devices: 48.4 us -> none  [local(): column = lax.all_gather(lhat_local, 'row', axis=0, tiled=True)]
    ppermute x0 -> x3, waiting for transfers between devices: none -> 33.4 us  [the longest x2 23.3 us: collect(): lax.ppermute(going_up, axis, [(d, (d + 1) % ways) for d in range(ways)])]
    all_gather x1, waiting for transfers between devices: 25.2 us -> 0.02 us  [local(): sigma_rows = lax.all_gather(ancestor_inv, 'col', axis=1, tiled=True)]
    all_gather x1, waiting for transfers between devices: 33.7 us -> 21.9 us  [local(): rows_all = lax.all_gather(lhat_local, 'col', axis=1, tiled=True)]
    ppermute x0 -> x3, starting transfers between devices: none -> 5.17 us  [the longest x2 3.08 us: collect(): lax.ppermute(going_up, axis, [(d, (d + 1) % ways) for d in range(ways)])]
  transfers between devices with their start and end apart: 4 -> 6, of which waited for: 4 -> 5; matrix products, arithmetic and copies ran while one was open for 3% -> 3% of each run, Pallas kernels for 0% -> 0%
where the time goes in v2:
time: 391 us
  waiting for transfers between devices  330 us (84%)
  local copies, waits for them, and re-layouts  17.4 us (4%)
  other arithmetic  14 us (4%)
  between operations  13.8 us (4%)
  matrix products  10.4 us (3%)
  starting transfers between devices  5.29 us (1%)
    reduce_scatter x1, waiting for transfers between devices, local(): lax.psum_scatter(jnp.concatenate(pieces, axis=1), 'row', scatter_dimensio...  274 us
    ppermute x2, waiting for transfers between devices, collect(): lax.ppermute(going_up, axis, [(d, (d + 1) % ways) for d in range(ways)])  23.3 us
    all_gather x1, waiting for transfers between devices, local(): rows_all = lax.all_gather(lhat_local, 'col', axis=1, tiled=True)  21.9 us
    unnamed x10, local copies, waits for them, and re-layouts  13.3 us
    ppermute x1, waiting for transfers between devices, collect(): lax.ppermute(going_down, axis, [(d, (d - 1) % ways) for d in range(ways)])  10 us
  transfers between devices with their start and end apart: 6, of which 5 were waited for; matrix products, arithmetic and copies ran while one was open for 3% of the time, Pallas kernels for 0%

profile of v2, /device:TPU:0, one launch (start us, length us, event | category | flops | bytes accessed | tf_op | source)
XLA Modules:
  0.0 390.8 jit_solution(5213848980744734588)
XLA Ops:
  7.2 0.7 all-gather.3.cloned.1.call-update
  8.0 0.1 broadcast_bitcast_fusion
  8.1 1.2 copy.6
  9.3 0.3 broadcast_in_dim.17
  9.6 0.9 constant_dynamic-update-slice_fusion.3
  10.6 3.1 collective-permute-start
  13.7 2.1 collective-permute-start.1
  15.8 12.9 %collective-permute-done = bf16[256,1024]{0,1:T(8,128)(2,1)S(1)} collective-permute-done((bf16[256,1024]{0,1:T(8,128)(2,1)}, bf16[256,1024]{0,1:T(8,128)(2,1)S(1)}, u32[]{:S(2)}, u32[]{:S(2)}) %collective-permute-start) | collective-permute-done | bytes 524320 | tf_op jit(solution)/shard_map/ppermute | solution.py:18
  28.7 0.1 constant_dynamic-update-slice_fusion.2
  28.8 10.0 %collective-permute-done.1 = bf16[256,1024]{0,1:T(8,128)(2,1)} collective-permute-done((bf16[256,1024]{0,1:T(8,128)(2,1)}, bf16[256,1024]{0,1:T(8,128)(2,1)}, u32[]{:S(2)}, u32[]{:S(2)}) %collective-permute-start.1) | collective-permute-done | bytes 524320 | tf_op jit(solution)/shard_map/ppermute | solution.py:21
  38.8 1.1 constant_dynamic-update-slice_fusion.1
  39.9 10.4 %collective-permute-done.2 = bf16[256,1024]{0,1:T(8,128)(2,1)S(1)} collective-permute-done((bf16[256,1024]{0,1:T(8,128)(2,1)S(1)}, bf16[256,1024]{0,1:T(8,128)(2,1)S(1)}, u32[]{:S(2)}, u32[]{:S(2)}) %collective-permute-start.2) | collective-permute-done | bytes 524320 | tf_op jit(solution)/shard_map/ppermute | solution.py:18
  50.4 0.1 constant_dynamic-update-slice_fusion
  50.4 3.1 bitcast_select_fusion
  53.5 21.9 %all-gather.5.cloned.1.call-done = bf16[256,8192]{0,1:T(8,128)(2,1)} async-done(((bf16[256,1024]{0,1:T(8,128)(2,1)}), bf16[256,8192]{0,1:T(8,128)(2,1)}) %all-gather.5.cloned.1.call-update) | async-done | bytes 4194320 | tf_op jit(solution)/shard_map/all_gather | solution.py:41
  75.4 2.6 fusion.5
  78.0 3.6 fusion.3
  81.6 3.7 fusion.1
  85.3 6.3 %pad_maximum_fusion = f32[4096,1024]{0,1:T(8,128)} fusion(f32[4096,512]{0,1:T(8,128)S(1)} %fusion.1, f32[4096,512]{0,1:T(8,128)S(1)} %fusion.3), kind=kLoop, calls=%fused_computation | loop fusion | flops 4194304 | bytes 33554432 | tf_op jit(solution)/shard_map/concatenate | solution.py:62
  91.6 5.3 %copy.7 = f32[1024,1024]{0,1:T(8,128)} copy(f32[1024,1024]{1,0:T(8,128)} %param.6) | data formatting | bytes 8388608 | tf_op args[2]
  97.0 1.3 copy.8
  98.3 273.8 %reduce-scatter.2.cloned.1.call-done = f32[1024,1024]{0,1:T(8,128)} async-done(((f32[4096,1024]{0,1:T(8,128)}), f32[1024,1024]{0,1:T(8,128)}) %reduce-scatter.2.cloned.1.call-update) | async-done | bytes 4194320 | tf_op jit(solution)/shard_map/reduce_scatter | solution.py:61
  372.1 6.8 %sub.11 = f32[1024,1024]{0,1:T(8,128)} subtract(f32[1024,1024]{0,1:T(8,128)} %copy.7, f32[1024,1024]{0,1:T(8,128)} %reduce-scatter.2.cloned.1.call-done) | non-fusion elementwise | flops 1048576 | bytes 12582912 | tf_op jit(solution)/shard_map/sub | solution.py:64
  378.9 5.3 %copy.9 = f32[1024,1024]{1,0:T(8,128)} copy(f32[1024,1024]{0,1:T(8,128)} %sub.11) | data formatting | bytes 8388608
  (13 shorter events, 0.2 us)
Async XLA Ops:
  7.2 0.8 copy-start
  7.2 43.3 %all-gather.3.cloned.1.call-start = ((), (), s32[]{:S(2)}) async-start(), calls=%async_computation.1 | async-start | bytes 1179648 | tf_op jit(solution)/shard_map/all_gather | solution.py:37
  7.9 67.5 %all-gather.5.cloned.1.call-start = ((), (), s32[]{:S(2)}) async-start(), calls=%async_computation.2 | async-start | bytes 4718592 | tf_op jit(solution)/shard_map/all_gather | solution.py:41
  10.6 361.6 %reduce-scatter.2.cloned.1.call-start = ((), (), s32[]{:S(2)}) async-start(), calls=%async_computation.3 | async-start | bytes 20971520 | tf_op jit(solution)/shard_map/reduce_scatter | solution.py:61
  10.6 18.1 %collective-permute-start = (bf16[256,1024]{0,1:T(8,128)(2,1)}, bf16[256,1024]{0,1:T(8,128)(2,1)S(1)}, u32[]{:S(2)}, u32[]{:S(2)}) collective-permute-start(bf16[256,1024]{0,1:T(8,128)(2,1)} %get-tuple-element.7), channel_id=1, source_target_pairs={{0,8},{8,16},{16,24},{24,0},{1,9},{9,17},{17,25},{25,1},{2,10},{10... | collective-permute-start | bytes 1572872 | tf_op jit(solution)/shard_map/ppermute | solution.py:18
  13.7 25.2 %collective-permute-start.1 = (bf16[256,1024]{0,1:T(8,128)(2,1)}, bf16[256,1024]{0,1:T(8,128)(2,1)}, u32[]{:S(2)}, u32[]{:S(2)}) collective-permute-start(bf16[256,1024]{0,1:T(8,128)(2,1)} %get-tuple-element.7), channel_id=1, source_target_pairs={{0,24},{8,0},{16,8},{24,16},{1,25},{9,1},{17,9},{25,17},{2,26},{10... | collective-permute-start | bytes 1572872 | tf_op jit(solution)/shard_map/ppermute | solution.py:21
  28.7 21.6 %collective-permute-start.2 = (bf16[256,1024]{0,1:T(8,128)(2,1)S(1)}, bf16[256,1024]{0,1:T(8,128)(2,1)S(1)}, u32[]{:S(2)}, u32[]{:S(2)}) collective-permute-start(bf16[256,1024]{0,1:T(8,128)(2,1)S(1)} %collective-permute-done), channel_id=1, source_target_pairs={{0,8},{8,16},{16,24},{24,0},{1,9},{9,17},{17,25},{25,1},{2,10},{10... | collective-permute-start | bytes 1572872 | tf_op jit(solution)/shard_map/ppermute | solution.py:18
  378.9 5.4 %copy-start.1 = (s32[2,4]{1,0:T(2,128)S(1)}, s32[2,4]{1,0:T(2,128)}, u32[]{:S(2)}) copy-start(s32[2,4]{1,0:T(2,128)} %param.7) | copy-start | bytes 100
Sparse Core Ops, SparseCore 0:
  9.9 26.2 all-gather.2
  38.7 36.7 all-gather.4
  91.8 280.2 reduce-scatter.1
